TPU v7x, 32 devices: a whole 2x2x4 slice. The times are simulated.
32 devices in a mesh: site: 16 (over z, y, x), sec: 2 (over core).
Axes of the slice: x: 2, y: 2, z: 4, core: 2. Of those that a mesh axis runs over, the one named last changes fastest.
Arguments:
- env_in: float32 [16, 16, 256, 256], P('site', 'sec'), may hold values from -6 to 6
- ket: bfloat16 [16, 4, 16, 256, 256], P('site', None, 'sec'), may hold values from -0.1875 to 0.1875
- bra: bfloat16 [16, 4, 16, 256, 256], P('site', None, 'sec'), may hold values from -0.375 to 0.375
- source: int32 [16, 4, 16], P('site'), may hold values from 0 to 15, each once within a row
Outputs:
- env_out: float32 [16, 16, 256, 256], P('site', 'sec')
Inputs may be any that keep to these rules, and one draw needn't show every extreme that they name: For every site s and physical state p, source[s, p, :] is a permutation of the 16 sectors.
All inputs are finite; a program needn't handle non-finite values.
Results may differ from a plain program's by a relative error of at most 0.013.
Values may be sent and summed in bfloat16 or wider, within the bound.
A program may use at most 64 MiB of HBM per device.

v0:
```python
import jax
import jax.numpy as jnp
from jax import lax
from jax.sharding import PartitionSpec as P

ITERS = 4


def passed_along(block, axis, distance):
    devices = range(lax.axis_size(axis))
    route = [((i - distance) % len(devices), i) for i in devices]
    return lax.ppermute(block, axis, route)


def body(env_in, ket, bra, source):
    own_count = ket.shape[2]
    first = lax.axis_index("sec") * own_count
    own_source = lax.dynamic_slice_in_dim(source[0], first, own_count, 1)
    ket_local = ket[0]
    bra_local = bra[0]

    def advance(whole_low):
        picked = whole_low[own_source]
        half = jnp.einsum(
            "pbij,pbjk->pbik", picked, ket_local, preferred_element_type=jnp.float32
        ).astype(jnp.bfloat16)
        return jnp.einsum("pbji,pbjk->bik", bra_local, half, preferred_element_type=jnp.float32)

    whole_low = lax.all_gather(env_in.astype(jnp.bfloat16), "sec", axis=1, tiled=True)[0]
    following = advance(whole_low)
    for step in range(ITERS - 1):
        own_low = following.astype(jnp.bfloat16)[None]
        arrived = passed_along(own_low, "site", 1)
        whole_low = lax.all_gather(arrived, "sec", axis=1, tiled=True)[0]
        following = advance(whole_low)
    return passed_along(following[None], "site", 1)


def solution(mesh):
    in_specs = (
        P("site", "sec", None, None),
        P("site", None, "sec", None, None),
        P("site", None, "sec", None, None),
        P("site", None, None),
    )
    out_specs = P("site", "sec", None, None)
    return jax.shard_map(body, mesh=mesh, in_specs=in_specs, out_specs=out_specs, check_vma=False)
```

profile of v0, /device:TPU:0, one launch (start us, length us, event | category | flops | bytes accessed | tf_op | source)
XLA Modules:
  0.0 245.7 jit_solution(15213304477971498390)
XLA Ops:
  6.5 2.7 %bitcast_convert_fusion.3 = bf16[1,8,256,256]{3,2,0,1:T(8,128)(2,1)} fusion(f32[1,8,256,256]{3,2,1,0:T(8,128)} %param.4), kind=kLoop, calls=%fused_computation.31 | loop fusion | flops 524288 | bytes 3145728 | tf_op jit(solution)/shard_map/convert_element_type | solution.py:29
  9.2 0.0 all-gather.5.cloned.1.call-update
  9.3 0.0 all-gather.7.cloned.1.call-start
  9.3 0.1 compare_select_fusion
  9.4 0.1 reshape.31
  9.5 13.2 %all-gather.5.cloned.1.call-done = bf16[1,16,256,256]{3,2,0,1:T(8,128)(2,1)} async-done(((bf16[1,8,256,256]{3,2,0,1:T(8,128)(2,1)}), bf16[1,16,256,256]{3,2,0,1:T(8,128)(2,1)}) %all-gather.5.cloned.1.call-update) | async-done | bytes 2097168 | tf_op jit(solution)/shard_map/all_gather | solution.py:29
  22.7 4.4 %gather_fusion = bf16[32,256,256]{2,1,0:T(8,128)(2,1)} fusion(bf16[16,256,256]{2,1,0:T(8,128)(2,1)} %bitcast.78, s32[1024]{0:T(1024)S(1)} %pad_clamp_fusion), kind=kCustom, calls=%fused_computation | custom fusion | bytes 8388736 | tf_op jit(solution)/shard_map/gather | solution.py:23
  27.1 7.0 %fusion.89 = bf16[1,8,256,256]{2,3,1,0:T(8,128)(2,1)S(1)} fusion(bf16[4,8,256,256]{3,2,1,0:T(8,128)(2,1)} %bitcast.83, bf16[1,4,8,256,256]{4,3,2,1,0:T(8,128)(2,1)} %param.6, bf16[1,4,8,256,256]{4,3,2,1,0:T(8,128)(2,1)} %param.5), kind=kOutput, calls=%fused_computation.33 | convolution fusion | flops 2150105088 | bytes 13631488 | tf_op jit(solution)/shard_map/pbji,pbjk->bik/dot_general | solution.py:27
  34.1 1.8 collective-permute-start
  35.9 27.3 %collective-permute-done = bf16[1,8,256,256]{2,3,1,0:T(8,128)(2,1)S(1)} collective-permute-done((bf16[1,8,256,256]{2,3,1,0:T(8,128)(2,1)S(1)}, bf16[1,8,256,256]{2,3,1,0:T(8,128)(2,1)S(1)}, u32[]{:S(2)}, u32[]{:S(2)}) %collective-permute-start) | collective-permute-done | bytes 1048608 | tf_op jit(solution)/shard_map/ppermute | solution.py:12
  63.2 1.3 copy.12
  64.5 0.0 all-gather.7.cloned.1.call-update
  64.5 0.0 all-gather.9.cloned.1.call-start
  64.6 8.2 %all-gather.7.cloned.1.call-done = bf16[1,16,256,256]{3,2,0,1:T(8,128)(2,1)} async-done(((bf16[1,8,256,256]{3,2,0,1:T(8,128)(2,1)}), bf16[1,16,256,256]{3,2,0,1:T(8,128)(2,1)}) %all-gather.7.cloned.1.call-update) | async-done | bytes 2097168 | tf_op jit(solution)/shard_map/all_gather | solution.py:34
  72.8 4.4 %gather_fusion.1 = bf16[32,256,256]{2,1,0:T(8,128)(2,1)} fusion(bf16[16,256,256]{2,1,0:T(8,128)(2,1)} %bitcast.79, s32[1024]{0:T(1024)S(1)} %pad_clamp_fusion), kind=kCustom, calls=%fused_computation.1 | custom fusion | bytes 8388736 | tf_op jit(solution)/shard_map/gather | solution.py:23
  77.1 7.0 %fusion.98 = bf16[1,8,256,256]{2,3,1,0:T(8,128)(2,1)S(1)} fusion(bf16[4,8,256,256]{3,2,1,0:T(8,128)(2,1)} %bitcast.84, bf16[1,4,8,256,256]{4,3,2,1,0:T(8,128)(2,1)} %param.6, bf16[1,4,8,256,256]{4,3,2,1,0:T(8,128)(2,1)} %param.5), kind=kOutput, calls=%fused_computation.34 | convolution fusion | flops 2150105088 | bytes 13631488 | tf_op jit(solution)/shard_map/pbji,pbjk->bik/dot_general | solution.py:27
  84.2 1.8 collective-permute-start.1
  86.0 27.3 %collective-permute-done.1 = bf16[1,8,256,256]{2,3,1,0:T(8,128)(2,1)S(1)} collective-permute-done((bf16[1,8,256,256]{2,3,1,0:T(8,128)(2,1)S(1)}, bf16[1,8,256,256]{2,3,1,0:T(8,128)(2,1)S(1)}, u32[]{:S(2)}, u32[]{:S(2)}) %collective-permute-start.1) | collective-permute-done | bytes 1048608 | tf_op jit(solution)/shard_map/ppermute | solution.py:12
  113.3 1.3 copy.14
  114.6 0.0 all-gather.11.cloned.1.call-start
  114.7 8.2 %all-gather.9.cloned.1.call-done = bf16[1,16,256,256]{3,2,0,1:T(8,128)(2,1)} async-done(((bf16[1,8,256,256]{3,2,0,1:T(8,128)(2,1)}), bf16[1,16,256,256]{3,2,0,1:T(8,128)(2,1)}) %all-gather.9.cloned.1.call-update) | async-done | bytes 2097168 | tf_op jit(solution)/shard_map/all_gather | solution.py:34
  122.8 4.4 %gather_fusion.2 = bf16[32,256,256]{2,1,0:T(8,128)(2,1)} fusion(bf16[16,256,256]{2,1,0:T(8,128)(2,1)} %bitcast.80, s32[1024]{0:T(1024)S(1)} %pad_clamp_fusion), kind=kCustom, calls=%fused_computation.2 | custom fusion | bytes 8388736 | tf_op jit(solution)/shard_map/gather | solution.py:23
  127.2 7.0 %fusion.107 = bf16[1,8,256,256]{2,3,1,0:T(8,128)(2,1)S(1)} fusion(bf16[4,8,256,256]{3,2,1,0:T(8,128)(2,1)} %bitcast.85, bf16[1,4,8,256,256]{4,3,2,1,0:T(8,128)(2,1)} %param.6, bf16[1,4,8,256,256]{4,3,2,1,0:T(8,128)(2,1)} %param.5), kind=kOutput, calls=%fused_computation.35 | convolution fusion | flops 2150105088 | bytes 13631488 | tf_op jit(solution)/shard_map/pbji,pbjk->bik/dot_general | solution.py:27
  134.3 1.8 collective-permute-start.2
  136.1 27.3 %collective-permute-done.2 = bf16[1,8,256,256]{2,3,1,0:T(8,128)(2,1)S(1)} collective-permute-done((bf16[1,8,256,256]{2,3,1,0:T(8,128)(2,1)S(1)}, bf16[1,8,256,256]{2,3,1,0:T(8,128)(2,1)S(1)}, u32[]{:S(2)}, u32[]{:S(2)}) %collective-permute-start.2) | collective-permute-done | bytes 1048608 | tf_op jit(solution)/shard_map/ppermute | solution.py:12
  163.3 1.3 copy.16
  164.7 8.2 %all-gather.11.cloned.1.call-done = bf16[1,16,256,256]{3,2,0,1:T(8,128)(2,1)} async-done(((bf16[1,8,256,256]{3,2,0,1:T(8,128)(2,1)}), bf16[1,16,256,256]{3,2,0,1:T(8,128)(2,1)}) %all-gather.11.cloned.1.call-update) | async-done | bytes 2097168 | tf_op jit(solution)/shard_map/all_gather | solution.py:34
  172.9 4.4 %gather_fusion.3 = bf16[32,256,256]{2,1,0:T(8,128)(2,1)} fusion(bf16[16,256,256]{2,1,0:T(8,128)(2,1)} %bitcast.81, s32[1024]{0:T(1024)S(1)} %pad_clamp_fusion), kind=kCustom, calls=%fused_computation.3 | custom fusion | bytes 8388736 | tf_op jit(solution)/shard_map/gather | solution.py:23
  177.3 8.4 %fusion.56 = f32[1,8,256,256]{2,3,1,0:T(8,128)} fusion(bf16[4,8,256,256]{3,2,1,0:T(8,128)(2,1)} %bitcast.82, bf16[1,4,8,256,256]{4,3,2,1,0:T(8,128)(2,1)} %param.6, bf16[1,4,8,256,256]{4,3,2,1,0:T(8,128)(2,1)} %param.5), kind=kOutput, calls=%fused_computation.32 | convolution fusion | flops 2149580800 | bytes 14680064 | tf_op jit(solution)/shard_map/pbji,pbjk->bik/dot_general | solution.py:27
  185.6 1.7 collective-permute-start.3
  187.4 50.0 %collective-permute-done.3 = f32[1,8,256,256]{2,3,1,0:T(8,128)S(1)} collective-permute-done((f32[1,8,256,256]{2,3,1,0:T(8,128)}, f32[1,8,256,256]{2,3,1,0:T(8,128)S(1)}, u32[]{:S(2)}, u32[]{:S(2)}) %collective-permute-start.3) | collective-permute-done | bytes 2097184 | tf_op jit(solution)/shard_map/ppermute | solution.py:12
  237.3 1.8 copy.18
  (6 shorter events, 0.0 us)
Async XLA Ops:
  6.5 2.8 %copy-start = (s32[1,4,16]{2,1,0:T(4,128)S(1)}, s32[1,4,16]{2,1,0:T(4,128)}, u32[]{:S(2)}) copy-start(s32[1,4,16]{2,1,0:T(4,128)} %param.7) | copy-start | bytes 772
  6.5 16.2 %all-gather.5.cloned.1.call-start = ((), (), s32[]{:S(2)}) async-start(), calls=%async_computation | async-start | bytes 3145728 | tf_op jit(solution)/shard_map/all_gather | solution.py:29
  9.3 63.5 %all-gather.7.cloned.1.call-start = ((), (), s32[]{:S(2)}) async-start(), calls=%async_computation.1 | async-start | bytes 3145728 | tf_op jit(solution)/shard_map/all_gather | solution.py:34
  34.1 29.1 %collective-permute-start = (bf16[1,8,256,256]{2,3,1,0:T(8,128)(2,1)S(1)}, bf16[1,8,256,256]{2,3,1,0:T(8,128)(2,1)S(1)}, u32[]{:S(2)}, u32[]{:S(2)}) collective-permute-start(bf16[1,8,256,256]{2,3,1,0:T(8,128)(2,1)S(1)} %fusion.89), channel_id=1, source_target_pairs={{30,0},{0,2},{2,4},{4,6},{6,8},{8,10},{10,12},{12,14},{14,16},{16,... | collective-permute-start | bytes 3145736 | tf_op jit(solution)/shard_map/ppermute | solution.py:12
  64.5 58.3 %all-gather.9.cloned.1.call-start = ((), (), s32[]{:S(2)}) async-start(), calls=%async_computation.2 | async-start | bytes 3145728 | tf_op jit(solution)/shard_map/all_gather | solution.py:34
  84.2 29.1 %collective-permute-start.1 = (bf16[1,8,256,256]{2,3,1,0:T(8,128)(2,1)S(1)}, bf16[1,8,256,256]{2,3,1,0:T(8,128)(2,1)S(1)}, u32[]{:S(2)}, u32[]{:S(2)}) collective-permute-start(bf16[1,8,256,256]{2,3,1,0:T(8,128)(2,1)S(1)} %fusion.98), channel_id=1, source_target_pairs={{30,0},{0,2},{2,4},{4,6},{6,8},{8,10},{10,12},{12,14},{14,16},{16,... | collective-permute-start | bytes 3145736 | tf_op jit(solution)/shard_map/ppermute | solution.py:12
  114.6 58.3 %all-gather.11.cloned.1.call-start = ((), (), s32[]{:S(2)}) async-start(), calls=%async_computation.3 | async-start | bytes 3145728 | tf_op jit(solution)/shard_map/all_gather | solution.py:34
  134.3 29.1 %collective-permute-start.2 = (bf16[1,8,256,256]{2,3,1,0:T(8,128)(2,1)S(1)}, bf16[1,8,256,256]{2,3,1,0:T(8,128)(2,1)S(1)}, u32[]{:S(2)}, u32[]{:S(2)}) collective-permute-start(bf16[1,8,256,256]{2,3,1,0:T(8,128)(2,1)S(1)} %fusion.107), channel_id=1, source_target_pairs={{30,0},{0,2},{2,4},{4,6},{6,8},{8,10},{10,12},{12,14},{14,16},{16,... | collective-permute-start | bytes 3145736 | tf_op jit(solution)/shard_map/ppermute | solution.py:12
  185.6 51.7 %collective-permute-start.3 = (f32[1,8,256,256]{2,3,1,0:T(8,128)}, f32[1,8,256,256]{2,3,1,0:T(8,128)S(1)}, u32[]{:S(2)}, u32[]{:S(2)}) collective-permute-start(f32[1,8,256,256]{2,3,1,0:T(8,128)} %fusion.56), channel_id=1, source_target_pairs={{30,0},{0,2},{2,4},{4,6},{6,8},{8,10},{10,12},{12,14},{14,16},{16,... | collective-permute-start | bytes 6291464 | tf_op jit(solution)/shard_map/ppermute | solution.py:12
Sparse Core Ops, SparseCore 0:
  9.4 13.2 all-gather.4
  64.7 8.0 all-gather.6
  114.7 8.0 all-gather.8
  164.8 8.0 all-gather.10
where the time goes:
time: 246 us
  waiting for transfers between devices  170 us (69%)
  matrix products  29.5 us (12%)
  local copies, waits for them, and re-layouts  23.3 us (9%)
  between operations  13.2 us (5%)
  starting transfers between devices  7.23 us (3%)
  other arithmetic  2.77 us (1%)
    ppermute x4, waiting for transfers between devices, passed_along(): return lax.ppermute(block, axis, route)  132 us
    dot_general x4, matrix products, advance(): jnp.einsum('pbji,pbjk->bik', bra_local, half, preferred_element_type=jnp....  29.5 us
    all_gather x3, waiting for transfers between devices, body(): whole_low = lax.all_gather(arrived, 'sec', axis=1, tiled=True)[0]  24.6 us
    gather x4, local copies, waits for them, and re-layouts, advance(): picked = whole_low[own_source]  17.5 us
    all_gather x1, waiting for transfers between devices, body(): lax.all_gather(env_in.astype(jnp.bfloat16), 'sec', axis=1, tiled=True)[0]  13.2 us
    ppermute x4, starting transfers between devices, passed_along(): return lax.ppermute(block, axis, route)  7.1 us
    ppermute x4, local copies, waits for them, and re-layouts, passed_along(): return lax.ppermute(block, axis, route)  5.7 us
  transfers between devices with their start and end apart: 8, of which 8 were waited for; matrix products, arithmetic and copies ran while one was open for 0% of the time, Pallas kernels for 0%

commit v1 on v0

v1 whole, which is shorter than its diff:
```python
import functools

import jax
import jax.numpy as jnp
from jax import lax
from jax.experimental import pallas as pl
from jax.experimental.pallas import tpu as pltpu
from jax.sharding import PartitionSpec as P

ITERS = 4
MESH = pl.DeviceIdType.MESH


def kernel(
    sites, groups, source_ref, env_hbm, ket_hbm, bra_hbm, out_ref,
    env, ket, bra, bra_t, staged,
    env_sem, ket_sem, bra_sem, share_send, share_recv, hop_send, hop_recv, *low,
):
    site = lax.axis_index("site")
    sec = lax.axis_index("sec")
    states, own = ket.shape[0], ket.shape[1]
    first = sec * own
    after = lax.rem(site + 1, sites)
    before = lax.rem(site + sites - 1, sites)

    def sibling(k):
        return lax.rem(sec + k, groups)

    def load_env(b):
        return pltpu.make_async_copy(env_hbm.at[b], env.at[b], env_sem.at[b])

    def load_ket(b):
        return pltpu.make_async_copy(ket_hbm.at[:, b], ket.at[:, b], ket_sem.at[b])

    def load_bra(b):
        return pltpu.make_async_copy(bra_hbm.at[:, b], bra.at[:, b], bra_sem.at[b])

    def share(t, k, b):
        return pltpu.make_async_remote_copy(
            src_ref=low[t].at[first + b],
            dst_ref=low[t].at[first + b],
            send_sem=share_send.at[t, k - 1, b],
            recv_sem=share_recv.at[t, k - 1, b],
            device_id=(site, sibling(k)),
            device_id_type=MESH,
        )

    def shared(t, k, b):
        row = lax.rem(sec + groups - k, groups) * own + b
        return pltpu.make_async_remote_copy(
            src_ref=low[t].at[row],
            dst_ref=low[t].at[row],
            send_sem=share_send.at[t, k - 1, b],
            recv_sem=share_recv.at[t, k - 1, b],
            device_id=(site, sibling(k)),
            device_id_type=MESH,
        )

    def hop(t, b):
        return pltpu.make_async_remote_copy(
            src_ref=staged.at[t, b],
            dst_ref=low[t + 1].at[first + b] if t < ITERS - 1 else out_ref.at[b],
            send_sem=hop_send.at[t, b],
            recv_sem=hop_recv.at[t, b],
            device_id=(after, sec),
            device_id_type=MESH,
        )

    def each(body):
        def one(b, carry):
            body(b)
            return carry

        lax.fori_loop(0, own, one, 0)

    each(lambda b: load_env(b).start())
    each(lambda b: load_ket(b).start())
    each(lambda b: load_bra(b).start())

    barrier = pltpu.get_barrier_semaphore()
    for peer in [(after, sec), (before, sec)] + [(site, sibling(k)) for k in range(1, groups)]:
        pl.semaphore_signal(barrier, inc=1, device_id=peer, device_id_type=MESH)
    pl.semaphore_wait(barrier, groups + 1)

    def open_own(b):
        load_env(b).wait()
        low[0][first + b] = env[b].astype(jnp.bfloat16)
        for k in range(1, groups):
            share(0, k, b).start()

    each(open_own)

    def advance(t, b):
        total = None
        for p in range(states):
            if t == 0:
                bra_t[p, b] = bra[p, b].T
            picked = low[t][source_ref[p, first + b]]
            half = jnp.dot(picked, ket[p, b], preferred_element_type=jnp.float32).astype(jnp.bfloat16)
            term = jnp.dot(bra_t[p, b], half, preferred_element_type=jnp.float32)
            total = term if total is None else total + term
        staged[t, b] = total.astype(jnp.bfloat16)
        hop(t, b).start()

    for t in range(ITERS):
        if t > 0:

            def pass_on(b, t=t):
                hop(t - 1, b).wait_recv()
                for k in range(1, groups):
                    share(t, k, b).start()

            each(pass_on)

        def arrive(b, t=t):
            for k in range(1, groups):
                shared(t, k, b).wait_recv()

        each(arrive)

        def work(b, t=t):
            if t == 0:
                load_ket(b).wait()
                load_bra(b).wait()
            advance(t, b)

        each(work)

    def finish(b):
        for t in range(ITERS):
            hop(t, b).wait_send()
            for k in range(1, groups):
                share(t, k, b).wait_send()
        hop(ITERS - 1, b).wait_recv()

    each(finish)


def body(sites, groups, env_in, ket, bra, source):
    _, states, own, rows, cols = ket.shape
    whole = own * groups
    low = jnp.bfloat16
    arrived = pl.pallas_call(
        functools.partial(kernel, sites, groups),
        out_shape=jax.ShapeDtypeStruct((own, rows, cols), low),
        in_specs=[pl.BlockSpec(memory_space=pltpu.SMEM)] + [pl.BlockSpec(memory_space=pl.ANY)] * 3,
        out_specs=pl.BlockSpec(memory_space=pltpu.VMEM),
        scratch_shapes=[
            pltpu.VMEM((own, rows, cols), jnp.float32),
            pltpu.VMEM((states, own, rows, cols), low),
            pltpu.VMEM((states, own, rows, cols), low),
            pltpu.VMEM((states, own, rows, cols), low),
            pltpu.VMEM((ITERS, own, rows, cols), low),
            pltpu.SemaphoreType.DMA((own,)),
            pltpu.SemaphoreType.DMA((own,)),
            pltpu.SemaphoreType.DMA((own,)),
            pltpu.SemaphoreType.DMA((ITERS, groups - 1, own)),
            pltpu.SemaphoreType.DMA((ITERS, groups - 1, own)),
            pltpu.SemaphoreType.DMA((ITERS, own)),
            pltpu.SemaphoreType.DMA((ITERS, own)),
        ]
        + [pltpu.VMEM((whole, rows, cols), low)] * ITERS,
        compiler_params=pltpu.CompilerParams(collective_id=0, has_side_effects=True),
    )(source[0], env_in[0], ket[0], bra[0])
    return arrived.astype(jnp.float32)[None]


def solution(mesh):
    in_specs = (
        P("site", "sec", None, None),
        P("site", None, "sec", None, None),
        P("site", None, "sec", None, None),
        P("site", None, None),
    )
    out_specs = P("site", "sec", None, None)
    part = functools.partial(body, mesh.shape["site"], mesh.shape["sec"])
    return jax.shard_map(part, mesh=mesh, in_specs=in_specs, out_specs=out_specs, check_vma=False)
```

time: 246 us -> 120 us (0.49)
  waiting for transfers between devices: 170 us -> 0 us
  Pallas kernels: 0 us -> 117 us
  matrix products: 29.5 us -> 0 us
  local copies, waits for them, and re-layouts: 23.3 us -> 0 us
  between operations: 13.2 us -> 0.01 us
  starting transfers between devices: 7.23 us -> 0 us
    ppermute x4 -> x0, waiting for transfers between devices: 132 us -> none  [passed_along(): return lax.ppermute(block, axis, route)]
    pallas_call x0 -> x1, Pallas kernels: none -> 117 us  [body(): pl.pallas_call(functools.partial(kernel, sites, groups), out_shape=jax.Sh...]
    all_gather x4 -> x0, waiting for transfers between devices: 37.8 us -> none  [the longest x3 24.6 us: body(): whole_low = lax.all_gather(arrived, 'sec', axis=1, tiled=True)[0]]
    dot_general x4 -> x0, matrix products: 29.5 us -> none  [advance(): jnp.einsum('pbji,pbjk->bik', bra_local, half, preferred_element_type=jnp....]
    gather x4 -> x0, local copies, waits for them, and re-layouts: 17.5 us -> none  [advance(): picked = whole_low[own_source]]
    ppermute x4 -> x0, starting transfers between devices: 7.1 us -> none  [passed_along(): return lax.ppermute(block, axis, route)]
    ppermute x4 -> x0, local copies, waits for them, and re-layouts: 5.7 us -> none  [passed_along(): return lax.ppermute(block, axis, route)]
    broadcast_in_dim x0 -> x1, other arithmetic: none -> 2.73 us  [body(): return arrived.astype(jnp.float32)[None]]
  transfers between devices with their start and end apart: 8 -> 0, of which waited for: 8 -> 0; matrix products, arithmetic and copies ran while one was open for 0% -> 0% of each run, Pallas kernels for 0% -> 0%
where the time goes in v1:
time: 120 us
  Pallas kernels  117 us (98%)
  other arithmetic  2.73 us (2%)
    pallas_call x1, Pallas kernels, body(): pl.pallas_call(functools.partial(kernel, sites, groups), out_shape=jax.Sh...  117 us
    broadcast_in_dim x1, other arithmetic, body(): return arrived.astype(jnp.float32)[None]  2.73 us

profile of v1, /device:TPU:0, one launch (start us, length us, event | category | flops | bytes accessed | tf_op | source)
XLA Modules:
  0.0 119.9 jit_solution(2354197008538862047)
XLA Ops:
  0.0 117.2 %shard_map.46 = bf16[8,256,256]{2,1,0:T(8,128)(2,1)} custom-call(s32[4,16]{1,0:T(4,128)} %bitcast.10, f32[8,256,256]{2,1,0:T(8,128)} %bitcast.9, bf16[4,8,256,256]{3,2,1,0:T(8,128)(2,1)} %bitcast.7, bf16[4,8,256,256]{3,2,1,0:T(8,128)(2,1)} %bitcast.8), custom_call_target="tpu_custom_call" | custom-call | tf_op jit(solution)/shard_map/pallas_call | solution.py:143
  117.2 2.7 %bitcast_convert_fusion = f32[1,8,256,256]{3,2,1,0:T(8,128)} fusion(bf16[8,256,256]{2,1,0:T(8,128)(2,1)} %shard_map.46), kind=kLoop, calls=%fused_computation | loop fusion | flops 524288 | bytes 3145728 | tf_op jit(solution)/shard_map/broadcast_in_dim | solution.py:165

commit v2 on v1

--- a/solution.py
+++ b/solution.py
@@ -8,17 +8,18 @@
 from jax.sharding import PartitionSpec as P
 
 ITERS = 4
+PIECES = 2
 MESH = pl.DeviceIdType.MESH
 
 
 def kernel(
     sites, groups, source_ref, env_hbm, ket_hbm, bra_hbm, out_ref,
-    env, ket, bra, bra_t, staged,
+    env, ket, bra, bra_t, halves, staged,
     env_sem, ket_sem, bra_sem, share_send, share_recv, hop_send, hop_recv, *low,
 ):
     site = lax.axis_index("site")
     sec = lax.axis_index("sec")
-    states, own = ket.shape[0], ket.shape[1]
+    states, own, rows = ket.shape[:3]
     first = sec * own
     after = lax.rem(site + 1, sites)
     before = lax.rem(site + sites - 1, sites)
@@ -56,12 +57,13 @@
             device_id_type=MESH,
         )
 
-    def hop(t, b):
+    def hop(t, b, q):
+        part = pl.ds(q * rows // PIECES, rows // PIECES)
         return pltpu.make_async_remote_copy(
-            src_ref=staged.at[t, b],
-            dst_ref=low[t + 1].at[first + b] if t < ITERS - 1 else out_ref.at[b],
-            send_sem=hop_send.at[t, b],
-            recv_sem=hop_recv.at[t, b],
+            src_ref=staged.at[t, b, part],
+            dst_ref=low[t + 1].at[first + b, part] if t < ITERS - 1 else out_ref.at[b, part],
+            send_sem=hop_send.at[t, b, q],
+            recv_sem=hop_recv.at[t, b, q],
             device_id=(after, sec),
             device_id_type=MESH,
         )
@@ -91,22 +93,24 @@
     each(open_own)
 
     def advance(t, b):
-        total = None
         for p in range(states):
             if t == 0:
-                bra_t[p, b] = bra[p, b].T
+                bra_t[b, :, p * rows : (p + 1) * rows] = bra[p, b].T
             picked = low[t][source_ref[p, first + b]]
-            half = jnp.dot(picked, ket[p, b], preferred_element_type=jnp.float32).astype(jnp.bfloat16)
-            term = jnp.dot(bra_t[p, b], half, preferred_element_type=jnp.float32)
-            total = term if total is None else total + term
-        staged[t, b] = total.astype(jnp.bfloat16)
-        hop(t, b).start()
+            half = jnp.dot(picked, ket[p, b], preferred_element_type=jnp.float32)
+            halves[p * rows : (p + 1) * rows] = half.astype(jnp.bfloat16)
+        for q in range(PIECES):
+            part = pl.ds(q * rows // PIECES, rows // PIECES)
+            total = jnp.dot(bra_t[b, part], halves[...], preferred_element_type=jnp.float32)
+            staged[t, b, part] = total.astype(jnp.bfloat16)
+            hop(t, b, q).start()
 
     for t in range(ITERS):
         if t > 0:
 
             def pass_on(b, t=t):
-                hop(t - 1, b).wait_recv()
+                for q in range(PIECES):
+                    hop(t - 1, b, q).wait_recv()
                 for k in range(1, groups):
                     share(t, k, b).start()
 
@@ -128,10 +132,12 @@
 
     def finish(b):
         for t in range(ITERS):
-            hop(t, b).wait_send()
+            for q in range(PIECES):
+                hop(t, b, q).wait_send()
             for k in range(1, groups):
                 share(t, k, b).wait_send()
-        hop(ITERS - 1, b).wait_recv()
+        for q in range(PIECES):
+            hop(ITERS - 1, b, q).wait_recv()
 
     each(finish)
 
@@ -144,20 +150,21 @@
         functools.partial(kernel, sites, groups),
         out_shape=jax.ShapeDtypeStruct((own, rows, cols), low),
         in_specs=[pl.BlockSpec(memory_space=pltpu.SMEM)] + [pl.BlockSpec(memory_space=pl.ANY)] * 3,
-        out_specs=pl.BlockSpec(memory_space=pltpu.VMEM),
+        out_specs=pl.BlockSpec(memory_space=pl.ANY),
         scratch_shapes=[
             pltpu.VMEM((own, rows, cols), jnp.float32),
             pltpu.VMEM((states, own, rows, cols), low),
             pltpu.VMEM((states, own, rows, cols), low),
-            pltpu.VMEM((states, own, rows, cols), low),
+            pltpu.VMEM((own, cols, states * rows), low),
+            pltpu.VMEM((states * rows, cols), low),
             pltpu.VMEM((ITERS, own, rows, cols), low),
             pltpu.SemaphoreType.DMA((own,)),
             pltpu.SemaphoreType.DMA((own,)),
             pltpu.SemaphoreType.DMA((own,)),
             pltpu.SemaphoreType.DMA((ITERS, groups - 1, own)),
             pltpu.SemaphoreType.DMA((ITERS, groups - 1, own)),
-            pltpu.SemaphoreType.DMA((ITERS, own)),
-            pltpu.SemaphoreType.DMA((ITERS, own)),
+            pltpu.SemaphoreType.DMA((ITERS, own, PIECES)),
+            pltpu.SemaphoreType.DMA((ITERS, own, PIECES)),
         ]
         + [pltpu.VMEM((whole, rows, cols), low)] * ITERS,
         compiler_params=pltpu.CompilerParams(collective_id=0, has_side_effects=True),

time: 120 us -> 119 us (level)
  no operation moved by 1% of the time
where the time goes in v2:
time: 119 us
  Pallas kernels  116 us (97%)
  other arithmetic  2.73 us (2%)
    pallas_call x1, Pallas kernels, body(): pl.pallas_call(functools.partial(kernel, sites, groups), out_shape=jax.Sh...  116 us
    broadcast_in_dim x1, other arithmetic, body(): return arrived.astype(jnp.float32)[None]  2.73 us

profile of v2, /device:TPU:0, one launch (start us, length us, event | category | flops | bytes accessed | tf_op | source)
XLA Modules:
  0.0 118.9 jit_solution(11444765261030556309)
XLA Ops:
  0.0 116.1 %shard_map.46 = bf16[8,256,256]{2,1,0:T(8,128)(2,1)} custom-call(s32[4,16]{1,0:T(4,128)} %bitcast.10, f32[8,256,256]{2,1,0:T(8,128)} %bitcast.9, bf16[4,8,256,256]{3,2,1,0:T(8,128)(2,1)} %bitcast.7, bf16[4,8,256,256]{3,2,1,0:T(8,128)(2,1)} %bitcast.8), custom_call_target="tpu_custom_call" | custom-call | tf_op jit(solution)/shard_map/pallas_call | solution.py:149
  116.1 2.7 %bitcast_convert_fusion = f32[1,8,256,256]{3,2,1,0:T(8,128)} fusion(bf16[8,256,256]{2,1,0:T(8,128)(2,1)} %shard_map.46), kind=kLoop, calls=%fused_computation | loop fusion | flops 524288 | bytes 3145728 | tf_op jit(solution)/shard_map/broadcast_in_dim | solution.py:172

commit v3 on v2

--- a/solution.py
+++ b/solution.py
@@ -75,13 +75,13 @@
 
         lax.fori_loop(0, own, one, 0)
 
+    barrier = pltpu.get_barrier_semaphore()
+    for peer in [(after, sec), (before, sec)] + [(site, sibling(k)) for k in range(1, groups)]:
+        pl.semaphore_signal(barrier, inc=1, device_id=peer, device_id_type=MESH)
+
     each(lambda b: load_env(b).start())
     each(lambda b: load_ket(b).start())
     each(lambda b: load_bra(b).start())
-
-    barrier = pltpu.get_barrier_semaphore()
-    for peer in [(after, sec), (before, sec)] + [(site, sibling(k)) for k in range(1, groups)]:
-        pl.semaphore_signal(barrier, inc=1, device_id=peer, device_id_type=MESH)
     pl.semaphore_wait(barrier, groups + 1)
 
     def open_own(b):

time: 119 us -> 119 us (level)
  no operation moved by 1% of the time
where the time goes in v3:
time: 119 us
  Pallas kernels  116 us (97%)
  other arithmetic  2.73 us (2%)
    pallas_call x1, Pallas kernels, body(): pl.pallas_call(functools.partial(kernel, sites, groups), out_shape=jax.Sh...  116 us
    broadcast_in_dim x1, other arithmetic, body(): return arrived.astype(jnp.float32)[None]  2.73 us

profile of v3, /device:TPU:0, one launch (start us, length us, event | category | flops | bytes accessed | tf_op | source)
XLA Modules:
  0.0 118.7 jit_solution(6383788206423201096)
XLA Ops:
  0.0 116.0 %shard_map.46 = bf16[8,256,256]{2,1,0:T(8,128)(2,1)} custom-call(s32[4,16]{1,0:T(4,128)} %bitcast.10, f32[8,256,256]{2,1,0:T(8,128)} %bitcast.9, bf16[4,8,256,256]{3,2,1,0:T(8,128)(2,1)} %bitcast.7, bf16[4,8,256,256]{3,2,1,0:T(8,128)(2,1)} %bitcast.8), custom_call_target="tpu_custom_call" | custom-call | tf_op jit(solution)/shard_map/pallas_call | solution.py:149
  116.0 2.7 %bitcast_convert_fusion = f32[1,8,256,256]{3,2,1,0:T(8,128)} fusion(bf16[8,256,256]{2,1,0:T(8,128)(2,1)} %shard_map.46), kind=kLoop, calls=%fused_computation | loop fusion | flops 524288 | bytes 3145728 | tf_op jit(solution)/shard_map/broadcast_in_dim | solution.py:172
